TPU v7x, 256 devices: a whole 4x4x8 slice. The times are simulated.
256 devices in a mesh: section: 16 (over y_hi, x, core), tensor: 16 (over y_lo, z).
Axes of the slice: x: 4, y: 4 (y_hi: 2, y_lo: 2; y = y_hi * 2 + y_lo), z: 8, core: 2. Of those that a mesh axis runs over, the one named last changes fastest.
Arguments:
- state: bfloat16 [16, 256, 6144], P('section', None, 'tensor'), may hold values from -6 to 6
- ln_gain: float32 [16, 6144], P('section'), may hold values from 0.1 to 1.9
- w_qkv: bfloat16 [16, 6144, 3, 4096], P('section', None, None, 'tensor'), may hold values from -0.078125 to 0.078125
- qk_gain: float32 [16, 2, 128], P('section'), may hold values from 0.5 to 1.5
- w_out: bfloat16 [16, 4096, 6144], P('section', 'tensor'), may hold values from -1 to 1
Outputs:
- advanced: bfloat16 [16, 256, 6144], P('section', None, 'tensor')
All inputs are finite; a program needn't handle non-finite values.
Results may differ from a plain program's by a relative error of at most 0.03.
Values may be sent and summed in bfloat16 or wider, within the bound.
No kernel may reach another device: no remote copies, remote signals or barrier semaphores. Data moves between devices by JAX's collectives and lax.ppermute only.
A program may use at most 128 MiB of HBM per device.

v0:
```python
import jax
import jax.numpy as jnp
from jax import lax
from jax.sharding import PartitionSpec as P

HD = 128
STEPS = 2


def passed_along(shard, axis, by):
    peers = lax.axis_size(axis)
    return lax.ppermute(shard, axis, [(i, (i + by) % peers) for i in range(peers)])


def layer_norm(values, gain):
    mean = jnp.mean(values, axis=-1, keepdims=True)
    squares = jnp.mean(values * values, axis=-1, keepdims=True)
    spread = squares - mean * mean
    return (values - mean) * lax.rsqrt(spread + 1e-06) * gain


def on_device(state, ln_gain, w_qkv, qk_gain, w_out):
    current = state[0]
    patches = current.shape[0]
    full_width = w_qkv.shape[1]
    head_cols = w_qkv.shape[3]
    local_heads = head_cols // HD
    qkv_flat = w_qkv[0].reshape(full_width, 3 * head_cols)
    out_local = w_out[0]
    gain_row = ln_gain[0]
    norm_gains = qk_gain[0]
    for step_index in range(STEPS):
        gathered = lax.all_gather(current, "tensor", axis=1, tiled=True)
        normed = layer_norm(gathered.astype(jnp.float32), gain_row).astype(jnp.bfloat16)
        projected = jnp.dot(normed, qkv_flat, preferred_element_type=jnp.float32)
        projected = projected.reshape(patches, 3, local_heads, HD)
        query = layer_norm(projected[:, 0], norm_gains[0]).astype(jnp.bfloat16)
        keys_all = layer_norm(projected[:, 1], norm_gains[1]).astype(jnp.bfloat16)
        value = projected[:, 2].astype(jnp.bfloat16)
        scores = jnp.einsum(
            "phe,qhe->hpq", query, keys_all, preferred_element_type=jnp.float32
        ) / jnp.sqrt(jnp.float32(HD))
        expo = jnp.exp(scores)
        attend = (expo / jnp.sum(expo, axis=-1, keepdims=True)).astype(jnp.bfloat16)
        mixed_rows = jnp.einsum("hpq,qhe->phe", attend, value, preferred_element_type=jnp.float32)
        mixed_rows = mixed_rows.astype(jnp.bfloat16).reshape(patches, head_cols)
        branch = lax.psum_scatter(
            lax.dot_general(
                out_local, mixed_rows, (((0,), (1,)), ((), ())), preferred_element_type=jnp.float32
            ).astype(jnp.bfloat16),
            "tensor",
            scatter_dimension=0,
            tiled=True,
        ).astype(jnp.float32)
        renewed = (current.astype(jnp.float32) + branch.T).astype(jnp.bfloat16)
        current = passed_along(renewed, "section", 1)
    return current[None]


def solution(mesh):
    placed = (
        P("section", None, "tensor"),
        P("section", None),
        P("section", None, None, "tensor"),
        P("section", None, None),
        P("section", "tensor", None),
    )
    return jax.shard_map(
        on_device,
        mesh=mesh,
        in_specs=placed,
        out_specs=P("section", None, "tensor"),
        check_vma=False,
    )
```

profile of v0, /device:TPU:16, one launch (start us, length us, event | category | flops | bytes accessed | tf_op | source)
XLA Modules:
  0.0 375.9 jit_solution(2082185066389066385)
XLA Ops:
  6.5 0.0 copy-start
  6.5 0.0 all-gather.6.cloned.1.call-start
  6.5 0.7 all-gather.6.cloned.1.call-update
  7.3 0.0 copy-start.7
  7.3 0.0 reduce-scatter.7.cloned.1.call-start
  7.3 12.9 %copy.19 = bf16[1,6144,3,256]{1,3,2,0:T(8,128)(2,1)} copy(bf16[1,6144,3,256]{3,1,2,0:T(8,128)(2,1)} %param.7) | data formatting | bytes 18874368 | tf_op args[2]
  20.2 0.0 copy-done.7
  20.2 0.0 copy-start.8
  20.2 65.4 %all-gather.6.cloned.1.call-done = bf16[1,256,6144]{2,1,0:T(8,128)(2,1)} async-done(((bf16[1,256,384]{2,1,0:T(8,128)(2,1)}), bf16[1,256,6144]{2,1,0:T(8,128)(2,1)}) %all-gather.6.cloned.1.call-update) | async-done | bytes 3145744 | tf_op jit(solution)/shard_map/all_gather | solution.py:33
  85.6 0.0 copy-start.1
  85.6 2.5 convert_reduce_fusion.1
  88.2 2.6 fusion.4
  90.8 0.0 copy-done.8
  90.8 0.0 copy-done.1
  90.8 6.0 %fusion.16 = f32[256,3,2,128]{0,3,2,1:T(8,128)S(1)} fusion(bf16[3,2,128,6144]{3,2,1,0:T(8,128)(2,1)} %bitcast.124, bf16[1,256,6144]{2,1,0:T(8,128)(2,1)S(1)} %copy-done.1, f32[6144]{0:T(1024)S(1)} %bitcast.130, f32[256]{0:T(256)S(1)} %get-tuple-element.28, f32[256]{0:T(256)S(1)} %get-tuple-element.27), kind=kOutput, calls=%fused_computation.22 | convolution fusion | flops 2423783424 | bytes 13395968 | tf_op jit(solution)/shard_map/dot_general | solution.py:35
  96.8 0.0 copy-start.3
  96.8 0.1 fusion.45
  96.9 0.7 copy-done.3
  97.6 1.2 fusion.27
  98.8 1.5 convolution_convert_fusion.3
  100.3 0.0 copy-done
  100.3 2.7 fusion.2
  103.0 0.0 copy-start.4
  103.0 4.7 %copy.34 = bf16[6144,256]{1,0:T(8,128)(2,1)} copy(bf16[6144,256]{0,1:T(8,128)(2,1)} %fusion.2) | data formatting | bytes 6291456
  107.7 0.0 reduce-scatter.7.cloned.1.call-update
  107.7 0.0 all-gather.4.cloned.1.call-start
  107.8 75.6 %reduce-scatter.7.cloned.1.call-done = bf16[384,256]{1,0:T(8,128)(2,1)} async-done(((bf16[6144,256]{1,0:T(8,128)(2,1)}), bf16[384,256]{1,0:T(8,128)(2,1)}) %reduce-scatter.7.cloned.1.call-update) | async-done | bytes 196624
  183.4 1.1 copy.35
  184.5 0.0 copy-done.4
  184.5 0.1 fusion.28
  184.6 0.1 collective-permute-start
  184.7 8.7 %collective-permute-done = bf16[256,384]{1,0:T(8,128)(2,1)S(1)} collective-permute-done((bf16[256,384]{1,0:T(8,128)(2,1)S(1)}, bf16[256,384]{1,0:T(8,128)(2,1)S(1)}, u32[]{:S(2)}, u32[]{:S(2)}) %collective-permute-start) | collective-permute-done | bytes 196640 | tf_op jit(solution)/shard_map/ppermute | solution.py:12
  193.4 0.0 copy-start.5
  193.4 0.7 copy-done.5
  194.0 0.0 all-gather.4.cloned.1.call-update
  194.1 0.0 reduce-scatter.9.cloned.1.call-start
  194.1 68.2 %all-gather.4.cloned.1.call-done = bf16[256,6144]{1,0:T(8,128)(2,1)} async-done(((bf16[256,384]{1,0:T(8,128)(2,1)}), bf16[256,6144]{1,0:T(8,128)(2,1)}) %all-gather.4.cloned.1.call-update) | async-done | bytes 3145744 | tf_op jit(solution)/shard_map/all_gather | solution.py:33
  262.3 3.2 convert_reduce_fusion
  265.5 6.5 %fusion.13 = f32[256,3,2,128]{0,3,2,1:T(8,128)S(1)} fusion(bf16[3,2,128,6144]{3,2,1,0:T(8,128)(2,1)} %bitcast.125, bf16[256,6144]{1,0:T(8,128)(2,1)} %all-gather.4.cloned.1.call-done, f32[256]{0:T(256)S(1)} %get-tuple-element.24, f32[256]{0:T(256)S(1)} %get-tuple-element.23, f32[6144]{0:T(1024)} %bitcast.129), kind=kOutput, calls=%fused_computation.20 | convolution fusion | flops 2423783424 | bytes 13395968 | tf_op jit(solution)/shard_map/dot_general | solution.py:35
  272.0 0.0 copy-start.2
  272.0 0.1 fusion.37
  272.2 0.7 copy-done.2
  272.9 1.1 fusion.26
  274.0 1.6 convolution_convert_fusion.2
  275.6 2.7 fusion.3
  278.3 0.0 copy-start.6
  278.3 4.7 %copy.36 = bf16[6144,256]{1,0:T(8,128)(2,1)} copy(bf16[6144,256]{0,1:T(8,128)(2,1)} %fusion.3) | data formatting | bytes 6291456
  283.0 0.0 reduce-scatter.9.cloned.1.call-update
  283.0 75.7 %reduce-scatter.9.cloned.1.call-done = bf16[384,256]{1,0:T(8,128)(2,1)} async-done(((bf16[6144,256]{1,0:T(8,128)(2,1)}), bf16[384,256]{1,0:T(8,128)(2,1)}) %reduce-scatter.9.cloned.1.call-update) | async-done | bytes 196624
  358.7 1.1 copy.37
  359.8 0.0 copy-done.6
  359.8 0.1 fusion.29
  359.9 0.1 collective-permute-start.1
  360.0 8.7 %collective-permute-done.1 = bf16[256,384]{1,0:T(8,128)(2,1)S(1)} collective-permute-done((bf16[256,384]{1,0:T(8,128)(2,1)S(1)}, bf16[256,384]{1,0:T(8,128)(2,1)S(1)}, u32[]{:S(2)}, u32[]{:S(2)}) %collective-permute-start.1) | collective-permute-done | bytes 196640 | tf_op jit(solution)/shard_map/ppermute | solution.py:12
  368.7 0.7 copy.39
  (8 shorter events, 0.2 us)
Async XLA Ops:
  6.5 93.8 %copy-start = (bf16[1,256,6144]{2,1,0:T(8,128)(2,1)S(1)}, bf16[1,256,6144]{2,1,0:T(8,128)(2,1)}, u32[]{:S(2)}) copy-start(bf16[1,256,6144]{2,1,0:T(8,128)(2,1)} %param.9) | copy-start | bytes 9437188
  6.5 79.1 %all-gather.6.cloned.1.call-start = ((), (), s32[]{:S(2)}) async-start(), calls=%async_computation.3 | async-start | bytes 3342336 | tf_op jit(solution)/shard_map/all_gather | solution.py:33
  7.3 12.9 %copy-start.7 = (f32[1,2,128]{2,1,0:T(2,128)S(1)}, f32[1,2,128]{2,1,0:T(2,128)}, u32[]{:S(2)}) copy-start(f32[1,2,128]{2,1,0:T(2,128)} %param.8) | copy-start | bytes 3076
  7.3 176.2 %reduce-scatter.7.cloned.1.call-start = ((), (), s32[]{:S(2)}) async-start(), calls=%async_computation.4 | async-start | bytes 3342336
  20.2 70.6 %copy-start.8 = (f32[1,6144]{1,0:T(1,128)S(1)}, f32[1,6144]{1,0:T(1,128)}, u32[]{:S(2)}) copy-start(f32[1,6144]{1,0:T(1,128)} %param.6) | copy-start | bytes 73732
  85.6 5.2 %copy-start.1 = (bf16[1,256,6144]{2,1,0:T(8,128)(2,1)S(1)}, bf16[1,256,6144]{2,1,0:T(8,128)(2,1)}, u32[]{:S(2)}) copy-start(bf16[1,256,6144]{2,1,0:T(8,128)(2,1)} %all-gather.6.cloned.1.call-done) | copy-start | bytes 9437188
  96.8 0.9 copy-start.3
  103.0 81.5 %copy-start.4 = (bf16[1,256,384]{2,1,0:T(8,128)(2,1)S(1)}, bf16[1,256,384]{2,1,0:T(8,128)(2,1)}, u32[]{:S(2)}) copy-start(bf16[1,256,384]{2,1,0:T(8,128)(2,1)} %param.5) | copy-start | bytes 589828
  107.7 154.6 %all-gather.4.cloned.1.call-start = ((), (), s32[]{:S(2)}) async-start(), calls=%async_computation.2 | async-start | bytes 3342336 | tf_op jit(solution)/shard_map/all_gather | solution.py:33
  184.6 8.8 %collective-permute-start = (bf16[256,384]{1,0:T(8,128)(2,1)S(1)}, bf16[256,384]{1,0:T(8,128)(2,1)S(1)}, u32[]{:S(2)}, u32[]{:S(2)}) collective-permute-start(bf16[256,384]{1,0:T(8,128)(2,1)S(1)} %fusion.28), channel_id=1, source_target_pairs={{0,16},{16,32},{32,48},{48,64},{64,80},{80,96},{96,112},{112,128},... | collective-permute-start | bytes 589832 | tf_op jit(solution)/shard_map/ppermute | solution.py:12
  193.4 0.7 copy-start.5
  194.1 164.6 %reduce-scatter.9.cloned.1.call-start = ((), (), s32[]{:S(2)}) async-start(), calls=%async_computation.5 | async-start | bytes 3342336
  272.0 0.9 copy-start.2
  278.3 81.5 %copy-start.6 = (bf16[256,384]{1,0:T(8,128)(2,1)S(1)}, bf16[256,384]{1,0:T(8,128)(2,1)}, u32[]{:S(2)}) copy-start(bf16[256,384]{1,0:T(8,128)(2,1)} %copy-done.5) | copy-start | bytes 589828
  359.9 8.8 %collective-permute-start.1 = (bf16[256,384]{1,0:T(8,128)(2,1)S(1)}, bf16[256,384]{1,0:T(8,128)(2,1)S(1)}, u32[]{:S(2)}, u32[]{:S(2)}) collective-permute-start(bf16[256,384]{1,0:T(8,128)(2,1)S(1)} %fusion.29), channel_id=1, source_target_pairs={{0,16},{16,32},{32,48},{48,64},{64,80},{80,96},{96,112},{112,128},... | collective-permute-start | bytes 589832 | tf_op jit(solution)/shard_map/ppermute | solution.py:12
Sparse Core Ops, SparseCore 0:
  9.2 76.4 all-gather.5
  107.8 75.5 reduce-scatter.6
  194.2 68.0 all-gather.3
  283.1 75.5 reduce-scatter.8
where the time goes:
time: 377 us; the launch traced here: 376 us
  waiting for transfers between devices  303 us (80%)
  local copies, waits for them, and re-layouts  27.3 us (7%)
  matrix products  23.2 us (6%)
  between operations  13.3 us (4%)
  other arithmetic  8.71 us (2%)
    unnamed x6, waiting for transfers between devices  152 us
    all_gather x2, waiting for transfers between devices, on_device(): gathered = lax.all_gather(current, 'tensor', axis=1, tiled=True)  134 us
    unnamed x24, local copies, waits for them, and re-layouts  27.3 us
    ppermute x2, waiting for transfers between devices, passed_along(): lax.ppermute(shard, axis, [(i, (i + by) % peers) for i in range(peers)])  17.4 us
    dot_general x2, matrix products, on_device(): projected = jnp.dot(normed, qkv_flat, preferred_element_type=jnp.float32)  12.5 us
  transfers between devices with their start and end apart: 6, of which 6 were waited for; matrix products, arithmetic and copies ran while one was open for 3% of the time, Pallas kernels for 0%

commit v1 on v0

--- a/solution.py
+++ b/solution.py
@@ -30,7 +30,9 @@
     gain_row = ln_gain[0]
     norm_gains = qk_gain[0]
     for step_index in range(STEPS):
-        gathered = lax.all_gather(current, "tensor", axis=1, tiled=True)
+        gathered = jnp.concatenate(
+            lax.all_to_all(jnp.stack([current] * lax.axis_size("tensor")), "tensor", 0, 0), axis=1
+        )
         normed = layer_norm(gathered.astype(jnp.float32), gain_row).astype(jnp.bfloat16)
         projected = jnp.dot(normed, qkv_flat, preferred_element_type=jnp.float32)
         projected = projected.reshape(patches, 3, local_heads, HD)

time: 377 us -> 395 us (1.048)
  waiting for transfers between devices: 303 us -> 230 us
  blocking collectives: 0 us -> 71.2 us
  local copies, waits for them, and re-layouts: 27.3 us -> 39.8 us
  starting transfers between devices: 0.29 us -> 9.71 us
    all_gather x2 -> x0, waiting for transfers between devices: 134 us -> none  [on_device(): gathered = lax.all_gather(current, 'tensor', axis=1, tiled=True)]
    all_to_all x0 -> x1, blocking collectives: none -> 71.2 us  [on_device(): lax.all_to_all(jnp.stack([current] * lax.axis_size('tensor')), 'tensor',...]
    all_to_all x0 -> x1, waiting for transfers between devices: none -> 57.2 us  [on_device(): lax.all_to_all(jnp.stack([current] * lax.axis_size('tensor')), 'tensor',...]
    all_to_all x0 -> x1, starting transfers between devices: none -> 9.46 us  [on_device(): lax.all_to_all(jnp.stack([current] * lax.axis_size('tensor')), 'tensor',...]
    all_to_all x0 -> x2, local copies, waits for them, and re-layouts: none -> 9.39 us  [on_device(): lax.all_to_all(jnp.stack([current] * lax.axis_size('tensor')), 'tensor',...]
    unnamed x6 -> x4, waiting for transfers between devices: 152 us -> 155 us
    unnamed x24 -> x27, local copies, waits for them, and re-layouts: 27.3 us -> 26.9 us
  transfers between devices with their start and end apart: 6 -> 5, of which waited for: 6 -> 5; matrix products, arithmetic and copies ran while one was open for 3% -> 4% of each run, Pallas kernels for 0% -> 0%
where the time goes in v1:
time: 395 us; the launch traced here: 394 us
  waiting for transfers between devices  230 us (58%)
  blocking collectives  71.2 us (18%)
  local copies, waits for them, and re-layouts  39.8 us (10%)
  matrix products  21.2 us (5%)
  between operations  13.6 us (3%)
  starting transfers between devices  9.71 us (2%)
  other arithmetic  9.15 us (2%)
    unnamed x4, waiting for transfers between devices  155 us
    all_to_all x1, blocking collectives, on_device(): lax.all_to_all(jnp.stack([current] * lax.axis_size('tensor')), 'tensor',...  71.2 us
    all_to_all x1, waiting for transfers between devices, on_device(): lax.all_to_all(jnp.stack([current] * lax.axis_size('tensor')), 'tensor',...  57.2 us
    unnamed x27, local copies, waits for them, and re-layouts  26.9 us
    ppermute x2, waiting for transfers between devices, passed_along(): lax.ppermute(shard, axis, [(i, (i + by) % peers) for i in range(peers)])  17.4 us
    dot_general x2, matrix products, on_device(): projected = jnp.dot(normed, qkv_flat, preferred_element_type=jnp.float32)  10.4 us
    all_to_all x1, starting transfers between devices, on_device(): lax.all_to_all(jnp.stack([current] * lax.axis_size('tensor')), 'tensor',...  9.46 us
    all_to_all x2, local copies, waits for them, and re-layouts, on_device(): lax.all_to_all(jnp.stack([current] * lax.axis_size('tensor')), 'tensor',...  9.39 us
  transfers between devices with their start and end apart: 5, of which 5 were waited for; matrix products, arithmetic and copies ran while one was open for 4% of the time, Pallas kernels for 0%

profile of v1, /device:TPU:16, one launch (start us, length us, event | category | flops | bytes accessed | tf_op | source)
XLA Modules:
  0.0 394.3 jit_solution(10069870483858540654)
XLA Ops:
  6.5 0.0 copy-start
  6.5 3.2 stack.4
  9.7 0.0 copy-start.8
  9.7 9.5 %all-to-all-start = ((bf16[16,256,384]{2,1,0:T(8,128)(2,1)}), bf16[16,256,384]{2,1,0:T(8,128)(2,1)}, u32[]{:S(2)}, u32[]{:S(2)}) async-start(bf16[16,256,384]{2,1,0:T(8,128)(2,1)} %stack.4), calls=%async_computation | async-start | bytes 6291456 | tf_op jit(solution)/shard_map/all_to_all | solution.py:34
  19.2 0.0 reduce-scatter.7.cloned.1.call-start
  19.2 0.5 broadcast.208
  19.7 0.0 copy-done.8
  19.7 0.7 reduce.15
  20.5 0.0 copy-start.6
  20.5 0.0 copy-start.9
  20.5 12.7 %copy.27 = bf16[1,6144,3,256]{1,3,2,0:T(8,128)(2,1)} copy(bf16[1,6144,3,256]{3,1,2,0:T(8,128)(2,1)} %param.7) | data formatting | bytes 18874368 | tf_op args[2]
  33.2 0.0 copy-done.9
  33.2 57.2 %all-to-all-done = bf16[16,256,384]{2,1,0:T(8,128)(2,1)} async-done(((bf16[16,256,384]{2,1,0:T(8,128)(2,1)}), bf16[16,256,384]{2,1,0:T(8,128)(2,1)}, u32[]{:S(2)}, u32[]{:S(2)}) %all-to-all-start) | async-done | bytes 3145760 | tf_op jit(solution)/shard_map/all_to_all | solution.py:34
  90.3 4.7 %copy.26 = bf16[16,256,384]{1,2,0:T(8,128)(2,1)} copy(bf16[16,256,384]{2,1,0:T(8,128)(2,1)} %all-to-all-done) | data formatting | bytes 6291456 | tf_op jit(solution)/shard_map/all_to_all | solution.py:34
  95.0 0.0 copy-start.2
  95.0 2.9 convert_reduce_fusion.1
  97.9 0.0 copy-done.6
  97.9 0.0 copy-done.2
  98.0 1.1 fusion.4
  99.1 5.2 %fusion.56 = f32[256,3,2,128]{0,3,2,1:T(8,128)S(1)} fusion(bf16[256,6144,1,1]{0,1,3,2:T(8,128)(2,1)S(1)} %bitcast.112, bf16[3,2,128,6144]{3,2,1,0:T(8,128)(2,1)} %bitcast.109), kind=kOutput, calls=%fused_computation.94 | convolution fusion | flops 2415919104 | bytes 13369344 | tf_op jit(solution)/shard_map/dot_general | solution.py:37
  104.3 0.0 copy-start.4
  104.4 0.1 fusion.31
  104.5 0.7 copy-done.4
  105.2 1.2 fusion.13
  106.4 1.5 convolution_convert_fusion.3
  107.9 0.0 copy-done
  107.9 2.7 fusion
  110.6 4.6 %copy.47 = bf16[6144,256]{1,0:T(8,128)(2,1)} copy(bf16[6144,256]{0,1:T(8,128)(2,1)} %fusion) | data formatting | bytes 6291456
  115.3 0.0 copy-start.5
  115.3 0.0 reduce-scatter.7.cloned.1.call-update
  115.3 0.0 reduce-scatter.9.cloned.1.call-start
  115.3 79.5 %reduce-scatter.7.cloned.1.call-done = bf16[384,256]{1,0:T(8,128)(2,1)} async-done(((bf16[6144,256]{1,0:T(8,128)(2,1)}), bf16[384,256]{1,0:T(8,128)(2,1)}) %reduce-scatter.7.cloned.1.call-update) | async-done | bytes 196624
  194.8 1.1 copy.48
  195.9 0.0 copy-done.5
  195.9 0.1 fusion.15
  196.0 0.1 collective-permute-start
  196.1 8.7 %collective-permute-done = bf16[256,384]{1,0:T(8,128)(2,1)S(1)} collective-permute-done((bf16[256,384]{1,0:T(8,128)(2,1)S(1)}, bf16[256,384]{1,0:T(8,128)(2,1)S(1)}, u32[]{:S(2)}, u32[]{:S(2)}) %collective-permute-start) | collective-permute-done | bytes 196640 | tf_op jit(solution)/shard_map/ppermute | solution.py:12
  204.8 0.4 stack.5
  205.2 71.2 %all_to_all.10 = bf16[16,256,384]{2,1,0:T(8,128)(2,1)} all-to-all(bf16[16,256,384]{2,1,0:T(8,128)(2,1)S(1)} %stack.5), channel_id=1, replica_groups=mesh['section'=16,'tensor'=16] {'tensor'}, dimensions={0} | all-to-all | bytes 6291456 | tf_op jit(solution)/shard_map/all_to_all | solution.py:34
  276.4 0.0 copy-start.7
  276.4 4.7 %copy.32 = bf16[16,256,384]{1,2,0:T(8,128)(2,1)} copy(bf16[16,256,384]{2,1,0:T(8,128)(2,1)} %all_to_all.10) | data formatting | bytes 6291456 | tf_op jit(solution)/shard_map/all_to_all | solution.py:34
  281.1 0.0 copy-start.1
  281.1 2.9 convert_reduce_fusion
  284.0 0.0 copy-done.7
  284.0 0.0 copy-done.1
  284.0 1.1 fusion.8
  285.2 5.2 %fusion.57 = f32[256,3,2,128]{0,3,2,1:T(8,128)S(1)} fusion(bf16[256,6144,1,1]{0,1,3,2:T(8,128)(2,1)S(1)} %bitcast.111, bf16[3,2,128,6144]{3,2,1,0:T(8,128)(2,1)} %bitcast.110), kind=kOutput, calls=%fused_computation.95 | convolution fusion | flops 2415919104 | bytes 13369344 | tf_op jit(solution)/shard_map/dot_general | solution.py:37
  290.4 0.0 copy-start.3
  290.4 0.1 fusion.23
  290.6 0.7 copy-done.3
  291.3 1.1 fusion.12
  292.4 1.6 convolution_convert_fusion.2
  294.0 2.7 fusion.1
  296.7 4.6 %copy.49 = bf16[6144,256]{1,0:T(8,128)(2,1)} copy(bf16[6144,256]{0,1:T(8,128)(2,1)} %fusion.1) | data formatting | bytes 6291456
  301.4 0.0 reduce-scatter.9.cloned.1.call-update
  301.4 75.5 %reduce-scatter.9.cloned.1.call-done = bf16[384,256]{1,0:T(8,128)(2,1)} async-done(((bf16[6144,256]{1,0:T(8,128)(2,1)}), bf16[384,256]{1,0:T(8,128)(2,1)}) %reduce-scatter.9.cloned.1.call-update) | async-done | bytes 196624
  376.8 1.1 copy.50
  377.9 0.1 fusion.14
  378.0 0.1 collective-permute-start.1
  378.1 8.7 %collective-permute-done.1 = bf16[256,384]{1,0:T(8,128)(2,1)S(1)} collective-permute-done((bf16[256,384]{1,0:T(8,128)(2,1)S(1)}, bf16[256,384]{1,0:T(8,128)(2,1)S(1)}, u32[]{:S(2)}, u32[]{:S(2)}) %collective-permute-start.1) | collective-permute-done | bytes 196640 | tf_op jit(solution)/shard_map/ppermute | solution.py:12
  386.8 0.7 copy.52
  (9 shorter events, 0.2 us)
Async XLA Ops:
  6.5 101.4 %copy-start = (bf16[1,256,6144]{2,1,0:T(8,128)(2,1)S(1)}, bf16[1,256,6144]{2,1,0:T(8,128)(2,1)}, u32[]{:S(2)}) copy-start(bf16[1,256,6144]{2,1,0:T(8,128)(2,1)} %param.9) | copy-start | bytes 9437188
  9.7 10.0 %copy-start.8 = (f32[1,6144]{1,0:T(1,128)S(1)}, f32[1,6144]{1,0:T(1,128)}, u32[]{:S(2)}) copy-start(f32[1,6144]{1,0:T(1,128)} %param.6) | copy-start | bytes 73732
  9.7 80.6 %all-to-all-start = ((bf16[16,256,384]{2,1,0:T(8,128)(2,1)}), bf16[16,256,384]{2,1,0:T(8,128)(2,1)}, u32[]{:S(2)}, u32[]{:S(2)}) async-start(bf16[16,256,384]{2,1,0:T(8,128)(2,1)} %stack.4), calls=%async_computation | async-start | bytes 6291456 | tf_op jit(solution)/shard_map/all_to_all | solution.py:34
  19.2 175.6 %reduce-scatter.7.cloned.1.call-start = ((), (), s32[]{:S(2)}) async-start(), calls=%async_computation.4 | async-start | bytes 3342336
  20.5 77.5 %copy-start.6 = (f32[16,384]{1,0:T(8,128)}, f32[16,384]{1,0:T(8,128)S(1)}, u32[]{:S(2)}) copy-start(f32[16,384]{1,0:T(8,128)S(1)} %mul.182) | copy-start | bytes 73732
  20.5 12.7 %copy-start.9 = (f32[1,2,128]{2,1,0:T(2,128)S(1)}, f32[1,2,128]{2,1,0:T(2,128)}, u32[]{:S(2)}) copy-start(f32[1,2,128]{2,1,0:T(2,128)} %param.8) | copy-start | bytes 3076
  95.0 2.9 copy-start.2
  104.3 0.9 copy-start.4
  115.3 80.7 %copy-start.5 = (bf16[1,256,384]{2,1,0:T(8,128)(2,1)S(1)}, bf16[1,256,384]{2,1,0:T(8,128)(2,1)}, u32[]{:S(2)}) copy-start(bf16[1,256,384]{2,1,0:T(8,128)(2,1)} %param.5) | copy-start | bytes 589828
  115.3 261.6 %reduce-scatter.9.cloned.1.call-start = ((), (), s32[]{:S(2)}) async-start(), calls=%async_computation.5 | async-start | bytes 3342336
  196.0 8.8 %collective-permute-start = (bf16[256,384]{1,0:T(8,128)(2,1)S(1)}, bf16[256,384]{1,0:T(8,128)(2,1)S(1)}, u32[]{:S(2)}, u32[]{:S(2)}) collective-permute-start(bf16[256,384]{1,0:T(8,128)(2,1)S(1)} %fusion.15), channel_id=1, source_target_pairs={{0,16},{16,32},{32,48},{48,64},{64,80},{80,96},{96,112},{112,128},... | collective-permute-start | bytes 589832 | tf_op jit(solution)/shard_map/ppermute | solution.py:12
  276.4 7.6 %copy-start.7 = (f32[16,384]{1,0:T(8,128)S(1)}, f32[16,384]{1,0:T(8,128)}, u32[]{:S(2)}) copy-start(f32[16,384]{1,0:T(8,128)} %copy-done.6) | copy-start | bytes 73732
  281.1 2.9 copy-start.1
  290.4 0.9 copy-start.3
  378.0 8.8 %collective-permute-start.1 = (bf16[256,384]{1,0:T(8,128)(2,1)S(1)}, bf16[256,384]{1,0:T(8,128)(2,1)S(1)}, u32[]{:S(2)}, u32[]{:S(2)}) collective-permute-start(bf16[256,384]{1,0:T(8,128)(2,1)S(1)} %fusion.14), channel_id=1, source_target_pairs={{0,16},{16,32},{32,48},{48,64},{64,80},{80,96},{96,112},{112,128},... | collective-permute-start | bytes 589832 | tf_op jit(solution)/shard_map/ppermute | solution.py:12
Sparse Core Ops, SparseCore 0:
  115.4 79.3 reduce-scatter.6
  301.5 75.3 reduce-scatter.8
